TPU v7x, 32 devices: a whole 2x2x4 slice. The times are simulated.
32 devices in a mesh: row: 8 (over z, core), col: 4 (over y, x).
Axes of the slice: x: 2, y: 2, z: 4, core: 2. Of those that a mesh axis runs over, the one named last changes fastest.
Arguments:
- rhs: bfloat16 [3, 8, 64, 256], P(None, 'row'), may hold values from -6 to 6
- dinv: bfloat16 [3, 8, 256, 256], P(None, 'row'), as said below
- tiles: bfloat16 [2, 8, 8, 256, 256], P(None, 'row', 'col'), may hold values from -0.09375 to 0.09375
- pattern: int32 [2, 2, 8, 8], P(None, None, 'row', 'col'), may hold values from 0 to 7, as said below
Outputs:
- solution: float32 [3, 8, 64, 256], P(None, 'row')
Inputs may be any that keep to these rules, and one draw needn't show every extreme that they name: pattern[0, l, p, t] = p; pattern[1, l, p, t] = j has (j) modulo the size of col equal to t // 2; positions may repeat, and repeated tiles add. `dinv`: lower triangular with a positive diagonal.
All inputs are finite; a program needn't handle non-finite values.
Results may differ from a plain program's by a relative error of at most 0.0055.
Values may be sent and summed in bfloat16 or wider, within the bound.
No kernel may reach another device: no remote copies, remote signals or barrier semaphores. Data moves between devices by JAX's collectives and lax.ppermute only.
A program may use at most 64 MiB of HBM per device.

v0:
```python
import jax
import jax.numpy as jnp
from jax import lax
from jax.sharding import PartitionSpec as P


def broadcast(block, axis, holder):
    block = jnp.where(lax.axis_index(axis) == holder, block, jnp.zeros_like(block))
    return lax.psum(block, axis)


def collect(rounded, mine_col, col_count, repeat):
    whole_level = lax.all_gather(rounded, "row", axis=0, tiled=True)
    shaped = whole_level.reshape((repeat, col_count) + rounded.shape)
    picked = lax.dynamic_index_in_dim(shaped, mine_col, 1, keepdims=False)
    return picked.reshape((-1,) + rounded.shape[1:])


def per_device(rhs, dinv, tiles, pattern):
    blocks = rhs.shape[1]
    levels_all = rhs.shape[0]
    col_count = lax.axis_size("col")
    row_count = lax.axis_size("row")
    repeat = row_count // col_count
    mine_row = lax.axis_index("row")
    mine_col = lax.axis_index("col")
    targets = pattern[0, :, 0, :] % blocks
    raw_cols = pattern[1, :, 0, :]
    sources = raw_cols // blocks // col_count * blocks + raw_cols % blocks
    row_pick = (targets[:, None, :] == jnp.arange(blocks, dtype=jnp.int32)[None, :, None]).astype(
        jnp.float32
    )
    col_pick = (
        sources[:, None, :] == jnp.arange(repeat * blocks, dtype=jnp.int32)[None, :, None]
    ).astype(jnp.float32)
    fronts = [rhs]
    forward_all = [[] for front in fronts]
    rounded_all = [None for front in fronts]
    for level_now in range(levels_all):
        front_index = 0
        front_level = fronts[front_index][level_now]
        current = front_level.astype(jnp.float32)
        if level_now > 0:
            nearby = collect(rounded_all[front_index], mine_col, col_count, repeat)
            source = jnp.take(nearby, sources[level_now - 1], axis=0)
            product = jnp.einsum(
                "sjb,sab->sja", source, tiles[level_now - 1, 0], preferred_element_type=jnp.float32
            )
            partial_value = jnp.sum(
                row_pick[level_now - 1][:, :, None, None] * product[None], axis=1
            )
            total_sum = lax.psum(partial_value, "col")
            current = current - total_sum
        solved = jnp.einsum(
            "rjb,rab->rja",
            current.astype(jnp.bfloat16),
            dinv[level_now],
            preferred_element_type=jnp.float32,
        )
        forward_all[front_index].append(solved)
        rounded_all[front_index] = solved.astype(jnp.bfloat16)
    backward_all = [[None] * levels_all for front in fronts]
    following_all = [None for front in fronts]
    for level_now in range(levels_all - 1, -1, -1):
        front_index = 0
        remainder = forward_all[front_index][level_now]
        if level_now < levels_all - 1:
            source = jnp.take(following_all[front_index], targets[level_now], axis=0)
            product = jnp.einsum(
                "sja,sab->sjb", source, tiles[level_now, 0], preferred_element_type=jnp.float32
            )
            partial_value = jnp.sum(col_pick[level_now][:, :, None, None] * product[None], axis=1)
            column_total = lax.psum(partial_value, "row")
            shaped = column_total.reshape((repeat, blocks) + column_total.shape[1:])
            picked = lax.dynamic_index_in_dim(shaped, mine_row // col_count, 0, keepdims=False)
            arrived = broadcast(picked, "col", mine_row % col_count)
            remainder = remainder - arrived
        solved = jnp.einsum(
            "rjb,rba->rja",
            remainder.astype(jnp.bfloat16),
            dinv[level_now],
            preferred_element_type=jnp.float32,
        )
        backward_all[front_index][level_now] = solved
        following_all[front_index] = solved.astype(jnp.bfloat16)
    front_index = 0
    levels_stack = jnp.stack(backward_all[front_index])
    return levels_stack


def solution(mesh):
    in_specs = (
        P(None, "row", None, None),
        P(None, "row", None, None),
        P(None, "row", "col", None, None),
        P(None, None, "row", "col"),
    )
    out_specs = P(None, "row", None, None)
    return jax.shard_map(
        per_device, mesh=mesh, in_specs=in_specs, out_specs=out_specs, check_vma=False
    )
```

profile of v0, /device:TPU:0, one launch (start us, length us, event | category | flops | bytes accessed | tf_op | source)
XLA Modules:
  0.0 337.1 jit_solution(15482950410898514648)
XLA Ops:
  6.5 1.1 fusion.57
  7.7 0.0 slice-start
  7.7 15.9 %all-gather = bf16[512,256]{1,0:T(8,128)(2,1)S(1)} all-gather(bf16[64,256]{1,0:T(8,128)(2,1)S(1)} %get-tuple-element.15), channel_id=2, replica_groups=mesh['row'=8,'col'=4] {'row'}, dimensions={0}, use_global_device_ids=true | all-gather | bytes 294912 | tf_op jit(solution)/shard_map/all_gather | solution.py:13
  23.7 0.6 gather_fusion
  24.3 0.8 convolution_bitcast_fusion.2
  25.1 0.0 all-reduce.7.cloned.1.call-update
  25.1 0.0 all-reduce.9.cloned.1.call-start
  25.2 43.0 %all-reduce.7.cloned.1.call-done = f32[1,64,256]{2,1,0:T(8,128)} async-done(((f32[1,64,256]{2,1,0:T(8,128)}), f32[1,64,256]{2,1,0:T(8,128)}) %all-reduce.7.cloned.1.call-update) | async-done | bytes 65552 | tf_op jit(solution)/shard_map/psum | solution.py:52
  68.2 1.0 fusion.58
  69.2 14.3 %all-gather.1 = bf16[512,256]{1,0:T(8,128)(2,1)S(1)} all-gather(bf16[64,256]{1,0:T(8,128)(2,1)S(1)} %get-tuple-element.17), channel_id=3, replica_groups=mesh['row'=8,'col'=4] {'row'}, dimensions={0}, use_global_device_ids=true | all-gather | bytes 294912 | tf_op jit(solution)/shard_map/all_gather | solution.py:13
  83.5 0.5 gather_fusion.1
  84.0 0.8 convolution_bitcast_fusion.1
  84.9 0.0 all-reduce.9.cloned.1.call-update
  84.9 0.0 all-reduce.11.cloned.1.call-start
  84.9 41.9 %all-reduce.9.cloned.1.call-done = f32[1,64,256]{2,1,0:T(8,128)} async-done(((f32[1,64,256]{2,1,0:T(8,128)}), f32[1,64,256]{2,1,0:T(8,128)}) %all-reduce.9.cloned.1.call-update) | async-done | bytes 65552 | tf_op jit(solution)/shard_map/psum | solution.py:52
  126.9 1.1 fusion.59
  128.0 0.2 fusion.1
  128.2 0.8 multiply_reduce_fusion.1
  128.9 0.0 all-reduce.13.cloned.1.call-start
  129.0 55.1 %all-reduce.11.cloned.1.call-done = f32[2,64,256]{2,1,0:T(8,128)} async-done(((f32[2,64,256]{2,1,0:T(8,128)}), f32[2,64,256]{2,1,0:T(8,128)}) %all-reduce.11.cloned.1.call-update) | async-done | bytes 131088 | tf_op jit(solution)/shard_map/psum | solution.py:73
  184.1 1.5 dynamic-slice_select_fusion.1
  185.6 0.0 all-reduce.15.cloned.1.call-start
  185.7 42.1 %all-reduce.13.cloned.1.call-done = f32[1,64,256]{2,1,0:T(8,128)} async-done(((f32[1,64,256]{2,1,0:T(8,128)}), f32[1,64,256]{2,1,0:T(8,128)}) %all-reduce.13.cloned.1.call-update) | async-done | bytes 65552 | tf_op jit(solution)/shard_map/psum | solution.py:9
  227.8 1.0 fusion.64
  228.8 0.2 fusion.4
  228.9 0.7 multiply_reduce_fusion
  229.7 0.0 all-reduce.17.cloned.1.call-start
  229.8 55.1 %all-reduce.15.cloned.1.call-done = f32[2,64,256]{2,1,0:T(8,128)} async-done(((f32[2,64,256]{2,1,0:T(8,128)}), f32[2,64,256]{2,1,0:T(8,128)}) %all-reduce.15.cloned.1.call-update) | async-done | bytes 131088 | tf_op jit(solution)/shard_map/psum | solution.py:73
  284.9 1.5 dynamic-slice_select_fusion
  286.4 42.2 %all-reduce.17.cloned.1.call-done = f32[1,64,256]{2,1,0:T(8,128)} async-done(((f32[1,64,256]{2,1,0:T(8,128)}), f32[1,64,256]{2,1,0:T(8,128)}) %all-reduce.17.cloned.1.call-update) | async-done | bytes 65552 | tf_op jit(solution)/shard_map/psum | solution.py:9
  328.5 1.0 convolution_bitcast_fusion
  329.5 0.7 pad_maximum_fusion
  (20 shorter events, 0.1 us)
Async XLA Ops:
  6.5 17.7 %copy-start.1 = (bf16[2,1,2,256,256]{4,3,2,1,0:T(8,128)(2,1)S(1)}, bf16[2,1,2,256,256]{4,3,2,1,0:T(8,128)(2,1)}, u32[]{:S(2)}) copy-start(bf16[2,1,2,256,256]{4,3,2,1,0:T(8,128)(2,1)} %param.10) | copy-start | bytes 1572868
  6.5 61.6 %all-reduce.7.cloned.1.call-start = ((), (), s32[]{:S(2)}) async-start(), calls=%async_computation | async-start | bytes 131072 | tf_op jit(solution)/shard_map/psum | solution.py:52
  7.7 16.0 %slice-start = ((s32[2,2,1,2]{3,2,1,0:T(1,128)}), s32[1,2,1,2]{3,2,1,0:T(1,128)S(1)}, s32[]{:S(2)}) async-start(s32[2,2,1,2]{3,2,1,0:T(1,128)} %param.11), calls=%async_computation.6 | async-start | bytes 2048 | tf_op jit(solution)/shard_map/slice | solution.py:28
  23.6 44.5 %copy-start = (bf16[3,1,256,256]{3,2,1,0:T(8,128)(2,1)S(1)}, bf16[3,1,256,256]{3,2,1,0:T(8,128)(2,1)}, u32[]{:S(2)}) copy-start(bf16[3,1,256,256]{3,2,1,0:T(8,128)(2,1)} %param.9) | copy-start | bytes 1179652
  24.3 43.9 %copy-start.2 = (bf16[3,1,64,256]{3,2,1,0:T(8,128)(2,1)S(1)}, bf16[3,1,64,256]{3,2,1,0:T(8,128)(2,1)}, u32[]{:S(2)}) copy-start(bf16[3,1,64,256]{3,2,1,0:T(8,128)(2,1)} %param.8) | copy-start | bytes 294916
  25.1 101.7 %all-reduce.9.cloned.1.call-start = ((), (), s32[]{:S(2)}) async-start(), calls=%async_computation.1 | async-start | bytes 131072 | tf_op jit(solution)/shard_map/psum | solution.py:52
  84.9 99.2 %all-reduce.11.cloned.1.call-start = ((), (), s32[]{:S(2)}) async-start(), calls=%async_computation.2 | async-start | bytes 262144 | tf_op jit(solution)/shard_map/psum | solution.py:73
  128.9 98.8 %all-reduce.13.cloned.1.call-start = ((), (), s32[]{:S(2)}) async-start(), calls=%async_computation.3 | async-start | bytes 131072 | tf_op jit(solution)/shard_map/psum | solution.py:9
  185.6 99.3 %all-reduce.15.cloned.1.call-start = ((), (), s32[]{:S(2)}) async-start(), calls=%async_computation.4 | async-start | bytes 262144 | tf_op jit(solution)/shard_map/psum | solution.py:73
  229.7 98.8 %all-reduce.17.cloned.1.call-start = ((), (), s32[]{:S(2)}) async-start(), calls=%async_computation.5 | async-start | bytes 131072 | tf_op jit(solution)/shard_map/psum | solution.py:9
Sparse Core Ops, SparseCore 0:
  25.3 42.8 all-reduce.6
  85.0 41.7 all-reduce.8
  129.2 54.9 all-reduce.10
  186.8 40.8 all-reduce.12
  229.9 54.9 all-reduce.14
  287.6 40.8 all-reduce.16
where the time goes:
time: 337 us
  waiting for transfers between devices  279 us (83%)
  blocking collectives  30.2 us (9%)
  between operations  13.6 us (4%)
  matrix products  7.25 us (2%)
  other arithmetic  5.19 us (2%)
    psum x2, waiting for transfers between devices, per_device(): column_total = lax.psum(partial_value, 'row')  110 us
    psum x2, waiting for transfers between devices, per_device(): total_sum = lax.psum(partial_value, 'col')  84.9 us
    psum x2, waiting for transfers between devices, broadcast(): return lax.psum(block, axis)  84.3 us
    all_gather x2, blocking collectives, collect(): whole_level = lax.all_gather(rounded, 'row', axis=0, tiled=True)  30.2 us
  transfers between devices with their start and end apart: 6, of which 6 were waited for; matrix products, arithmetic and copies ran while one was open for 0% of the time, Pallas kernels for 0%

commit v1 on v0

--- a/solution.py
+++ b/solution.py
@@ -10,7 +10,27 @@
 
 
 def collect(rounded, mine_col, col_count, repeat):
-    whole_level = lax.all_gather(rounded, "row", axis=0, tiled=True)
+    value_now = jax.lax.axis_size("row")
+    item_now = jax.lax.axis_index("row")
+    side_arr, r_now, x_now = (value_now, item_now, rounded.shape[0])
+    log = [(jj, (jj + 1) % side_arr) for jj in range(side_arr)]
+    row_list = [(jj, (jj - 1) % side_arr) for jj in range(side_arr)]
+    whole_level = jnp.zeros(
+        (*rounded.shape[:0], side_arr * x_now, *rounded.shape[1:]), rounded.dtype
+    )
+    whole_level = lax.dynamic_update_slice_in_dim(whole_level, rounded, r_now * x_now, axis=0)
+    aux = next_value = rounded
+    low = side_arr // 2
+    for ix in [*range(1, low + 1)]:
+        aux = jax.lax.ppermute(aux, "row", log)
+        whole_level = lax.dynamic_update_slice_in_dim(
+            whole_level, aux, (r_now - ix) % side_arr * x_now, axis=0
+        )
+        if ix < side_arr - low:
+            next_value = jax.lax.ppermute(next_value, "row", row_list)
+            whole_level = lax.dynamic_update_slice_in_dim(
+                whole_level, next_value, (r_now + ix) % side_arr * x_now, axis=0
+            )
     shaped = whole_level.reshape((repeat, col_count) + rounded.shape)
     picked = lax.dynamic_index_in_dim(shaped, mine_col, 1, keepdims=False)
     return picked.reshape((-1,) + rounded.shape[1:])

time: 337 us -> 345 us (1.024)
  blocking collectives: 30.2 us -> 0 us
  starting transfers between devices: 0.21 us -> 22.7 us
  waiting for transfers between devices: 279 us -> 294 us
    all_gather x2 -> x0, blocking collectives: 30.2 us -> none  [collect(): whole_level = lax.all_gather(rounded, 'row', axis=0, tiled=True)]
    ppermute x0 -> x14, starting transfers between devices: none -> 22.5 us  [the longest x6 21.9 us: collect(): next_value = jax.lax.ppermute(next_value, 'row', row_list)]
    ppermute x0 -> x14, waiting for transfers between devices: none -> 19.9 us  [the longest x8 19.8 us: collect(): aux = jax.lax.ppermute(aux, 'row', log)]
    psum x2, waiting for transfers between devices: 84.9 us -> 79.8 us  [per_device(): total_sum = lax.psum(partial_value, 'col')]
  transfers between devices with their start and end apart: 6 -> 20, of which waited for: 6 -> 15; matrix products, arithmetic and copies ran while one was open for 0% -> 0% of each run, Pallas kernels for 0% -> 0%
where the time goes in v1:
time: 345 us
  waiting for transfers between devices  294 us (85%)
  starting transfers between devices  22.7 us (7%)
  between operations  13.8 us (4%)
  matrix products  7.19 us (2%)
  other arithmetic  5.21 us (2%)
    psum x2, waiting for transfers between devices, per_device(): column_total = lax.psum(partial_value, 'row')  110 us
    psum x2, waiting for transfers between devices, broadcast(): return lax.psum(block, axis)  84.3 us
    psum x2, waiting for transfers between devices, per_device(): total_sum = lax.psum(partial_value, 'col')  79.8 us
    ppermute x6, starting transfers between devices, collect(): next_value = jax.lax.ppermute(next_value, 'row', row_list)  21.9 us
    ppermute x8, waiting for transfers between devices, collect(): aux = jax.lax.ppermute(aux, 'row', log)  19.8 us
  transfers between devices with their start and end apart: 20, of which 15 were waited for; matrix products, arithmetic and copies ran while one was open for 0% of the time, Pallas kernels for 0%

profile of v1, /device:TPU:0, one launch (start us, length us, event | category | flops | bytes accessed | tf_op | source)
XLA Modules:
  0.0 344.5 jit_solution(10908073853880852998)
XLA Ops:
  6.5 1.1 fusion.18
  8.3 4.1 %collective-permute-start.1 = (bf16[1,64,256]{2,1,0:T(8,128)(2,1)S(1)}, bf16[1,64,256]{2,1,0:T(8,128)(2,1)S(1)}, u32[]{:S(2)}, u32[]{:S(2)}) collective-permute-start(bf16[1,64,256]{2,1,0:T(8,128)(2,1)S(1)} %get-tuple-element.14), channel_id=1, source_target_pairs={{0,28},{4,0},{8,4},{12,8},{16,12},{20,16},{24,20},{28,24},{1,29},{... | collective-permute-start | bytes 98312 | tf_op jit(solution)/shard_map/ppermute | solution.py:30
  12.5 1.4 collective-permute-done
  13.9 3.5 %collective-permute-start.3 = (bf16[1,64,256]{2,1,0:T(8,128)(2,1)S(1)}, bf16[1,64,256]{2,1,0:T(8,128)(2,1)S(1)}, u32[]{:S(2)}, u32[]{:S(2)}) collective-permute-start(bf16[1,64,256]{2,1,0:T(8,128)(2,1)S(1)} %collective-permute-done.1), channel_id=1, source_target_pairs={{0,28},{4,0},{8,4},{12,8},{16,12},{20,16},{24,20},{28,24},{1,29},{... | collective-permute-start | bytes 98312 | tf_op jit(solution)/shard_map/ppermute | solution.py:30
  17.5 1.6 collective-permute-done.2
  19.1 3.5 %collective-permute-start.5 = (bf16[1,64,256]{2,1,0:T(8,128)(2,1)S(1)}, bf16[1,64,256]{2,1,0:T(8,128)(2,1)S(1)}, u32[]{:S(2)}, u32[]{:S(2)}) collective-permute-start(bf16[1,64,256]{2,1,0:T(8,128)(2,1)S(1)} %collective-permute-done.3), channel_id=1, source_target_pairs={{0,28},{4,0},{8,4},{12,8},{16,12},{20,16},{24,20},{28,24},{1,29},{... | collective-permute-start | bytes 98312 | tf_op jit(solution)/shard_map/ppermute | solution.py:30
  22.7 1.6 collective-permute-done.4
  24.3 5.1 %collective-permute-done.6 = bf16[1,64,256]{2,1,0:T(8,128)(2,1)S(1)} collective-permute-done((bf16[1,64,256]{2,1,0:T(8,128)(2,1)S(1)}, bf16[1,64,256]{2,1,0:T(8,128)(2,1)S(1)}, u32[]{:S(2)}, u32[]{:S(2)}) %collective-permute-start.6) | collective-permute-done | bytes 32800 | tf_op jit(solution)/shard_map/ppermute | solution.py:25
  30.0 0.8 convolution_bitcast_fusion.2
  30.9 40.6 %all-reduce.7.cloned.1.call-done = f32[1,64,256]{2,1,0:T(8,128)} async-done(((f32[1,64,256]{2,1,0:T(8,128)}), f32[1,64,256]{2,1,0:T(8,128)}) %all-reduce.7.cloned.1.call-update) | async-done | bytes 65552 | tf_op jit(solution)/shard_map/psum | solution.py:72
  71.5 1.0 fusion.15
  72.7 3.5 %collective-permute-start.8 = (bf16[1,64,256]{2,1,0:T(8,128)(2,1)S(1)}, bf16[1,64,256]{2,1,0:T(8,128)(2,1)S(1)}, u32[]{:S(2)}, u32[]{:S(2)}) collective-permute-start(bf16[1,64,256]{2,1,0:T(8,128)(2,1)S(1)} %get-tuple-element.10), channel_id=1, source_target_pairs={{0,28},{4,0},{8,4},{12,8},{16,12},{20,16},{24,20},{28,24},{1,29},{... | collective-permute-start | bytes 98312 | tf_op jit(solution)/shard_map/ppermute | solution.py:30
  76.2 1.7 collective-permute-done.7
  77.9 3.6 %collective-permute-start.10 = (bf16[1,64,256]{2,1,0:T(8,128)(2,1)S(1)}, bf16[1,64,256]{2,1,0:T(8,128)(2,1)S(1)}, u32[]{:S(2)}, u32[]{:S(2)}) collective-permute-start(bf16[1,64,256]{2,1,0:T(8,128)(2,1)S(1)} %collective-permute-done.8), channel_id=1, source_target_pairs={{0,28},{4,0},{8,4},{12,8},{16,12},{20,16},{24,20},{28,24},{1,29},{... | collective-permute-start | bytes 98312 | tf_op jit(solution)/shard_map/ppermute | solution.py:30
  81.5 1.9 collective-permute-done.9
  83.4 3.6 %collective-permute-start.12 = (bf16[1,64,256]{2,1,0:T(8,128)(2,1)S(1)}, bf16[1,64,256]{2,1,0:T(8,128)(2,1)S(1)}, u32[]{:S(2)}, u32[]{:S(2)}) collective-permute-start(bf16[1,64,256]{2,1,0:T(8,128)(2,1)S(1)} %collective-permute-done.10), channel_id=1, source_target_pairs={{0,28},{4,0},{8,4},{12,8},{16,12},{20,16},{24,20},{28,24},{1,29},{... | collective-permute-start | bytes 98312 | tf_op jit(solution)/shard_map/ppermute | solution.py:30
  87.0 1.5 collective-permute-done.11
  88.6 5.1 %collective-permute-done.13 = bf16[1,64,256]{2,1,0:T(8,128)(2,1)S(1)} collective-permute-done((bf16[1,64,256]{2,1,0:T(8,128)(2,1)S(1)}, bf16[1,64,256]{2,1,0:T(8,128)(2,1)S(1)}, u32[]{:S(2)}, u32[]{:S(2)}) %collective-permute-start.13) | collective-permute-done | bytes 32800 | tf_op jit(solution)/shard_map/ppermute | solution.py:25
  94.2 0.8 convolution_bitcast_fusion.1
  95.2 39.2 %all-reduce.9.cloned.1.call-done = f32[1,64,256]{2,1,0:T(8,128)} async-done(((f32[1,64,256]{2,1,0:T(8,128)}), f32[1,64,256]{2,1,0:T(8,128)}) %all-reduce.9.cloned.1.call-update) | async-done | bytes 65552 | tf_op jit(solution)/shard_map/psum | solution.py:72
  134.3 1.1 fusion.57
  135.6 0.8 multiply_reduce_fusion.1
  136.5 55.1 %all-reduce.11.cloned.1.call-done = f32[2,64,256]{2,1,0:T(8,128)} async-done(((f32[2,64,256]{2,1,0:T(8,128)}), f32[2,64,256]{2,1,0:T(8,128)}) %all-reduce.11.cloned.1.call-update) | async-done | bytes 131088 | tf_op jit(solution)/shard_map/psum | solution.py:93
  191.6 1.5 dynamic-slice_select_fusion.1
  193.1 42.1 %all-reduce.13.cloned.1.call-done = f32[1,64,256]{2,1,0:T(8,128)} async-done(((f32[1,64,256]{2,1,0:T(8,128)}), f32[1,64,256]{2,1,0:T(8,128)}) %all-reduce.13.cloned.1.call-update) | async-done | bytes 65552 | tf_op jit(solution)/shard_map/psum | solution.py:9
  235.2 1.0 fusion.62
  236.4 0.7 multiply_reduce_fusion
  237.2 55.1 %all-reduce.15.cloned.1.call-done = f32[2,64,256]{2,1,0:T(8,128)} async-done(((f32[2,64,256]{2,1,0:T(8,128)}), f32[2,64,256]{2,1,0:T(8,128)}) %all-reduce.15.cloned.1.call-update) | async-done | bytes 131088 | tf_op jit(solution)/shard_map/psum | solution.py:93
  292.3 1.5 dynamic-slice_select_fusion
  293.8 42.2 %all-reduce.17.cloned.1.call-done = f32[1,64,256]{2,1,0:T(8,128)} async-done(((f32[1,64,256]{2,1,0:T(8,128)}), f32[1,64,256]{2,1,0:T(8,128)}) %all-reduce.17.cloned.1.call-update) | async-done | bytes 65552 | tf_op jit(solution)/shard_map/psum | solution.py:9
  336.0 1.0 convolution_bitcast_fusion
  337.0 0.7 pad_maximum_fusion
  (64 shorter events, 2.8 us)
Async XLA Ops:
  6.5 65.0 %all-reduce.7.cloned.1.call-start = ((), (), s32[]{:S(2)}) async-start(), calls=%async_computation | async-start | bytes 131072 | tf_op jit(solution)/shard_map/psum | solution.py:72
  7.6 4.7 %slice-start = ((s32[2,2,1,2]{3,2,1,0:T(1,128)}), s32[1,2,1,2]{3,2,1,0:T(1,128)S(1)}, s32[]{:S(2)}) async-start(s32[2,2,1,2]{3,2,1,0:T(1,128)} %param.11), calls=%async_computation.6 | async-start | bytes 2048 | tf_op jit(solution)/shard_map/slice | solution.py:48
  7.7 22.3 %copy-start.1 = (bf16[2,1,2,256,256]{4,3,2,1,0:T(8,128)(2,1)S(1)}, bf16[2,1,2,256,256]{4,3,2,1,0:T(8,128)(2,1)}, u32[]{:S(2)}) copy-start(bf16[2,1,2,256,256]{4,3,2,1,0:T(8,128)(2,1)} %param.10) | copy-start | bytes 1572868
  7.7 6.2 %collective-permute-start = (bf16[1,64,256]{2,1,0:T(8,128)(2,1)S(1)}, bf16[1,64,256]{2,1,0:T(8,128)(2,1)S(1)}, u32[]{:S(2)}, u32[]{:S(2)}) collective-permute-start(bf16[1,64,256]{2,1,0:T(8,128)(2,1)S(1)} %get-tuple-element.14), channel_id=1, source_target_pairs={{0,4},{4,8},{8,12},{12,16},{16,20},{20,24},{24,28},{28,0},{1,5},{5... | collective-permute-start | bytes 98312 | tf_op jit(solution)/shard_map/ppermute | solution.py:25
  8.3 5.7 %collective-permute-start.1 = (bf16[1,64,256]{2,1,0:T(8,128)(2,1)S(1)}, bf16[1,64,256]{2,1,0:T(8,128)(2,1)S(1)}, u32[]{:S(2)}, u32[]{:S(2)}) collective-permute-start(bf16[1,64,256]{2,1,0:T(8,128)(2,1)S(1)} %get-tuple-element.14), channel_id=1, source_target_pairs={{0,28},{4,0},{8,4},{12,8},{16,12},{20,16},{24,20},{28,24},{1,29},{... | collective-permute-start | bytes 98312 | tf_op jit(solution)/shard_map/ppermute | solution.py:30
  13.9 5.2 %collective-permute-start.2 = (bf16[1,64,256]{2,1,0:T(8,128)(2,1)S(1)}, bf16[1,64,256]{2,1,0:T(8,128)(2,1)S(1)}, u32[]{:S(2)}, u32[]{:S(2)}) collective-permute-start(bf16[1,64,256]{2,1,0:T(8,128)(2,1)S(1)} %collective-permute-done), channel_id=1, source_target_pairs={{0,4},{4,8},{8,12},{12,16},{16,20},{20,24},{24,28},{28,0},{1,5},{5... | collective-permute-start | bytes 98312 | tf_op jit(solution)/shard_map/ppermute | solution.py:25
  13.9 5.2 %collective-permute-start.3 = (bf16[1,64,256]{2,1,0:T(8,128)(2,1)S(1)}, bf16[1,64,256]{2,1,0:T(8,128)(2,1)S(1)}, u32[]{:S(2)}, u32[]{:S(2)}) collective-permute-start(bf16[1,64,256]{2,1,0:T(8,128)(2,1)S(1)} %collective-permute-done.1), channel_id=1, source_target_pairs={{0,28},{4,0},{8,4},{12,8},{16,12},{20,16},{24,20},{28,24},{1,29},{... | collective-permute-start | bytes 98312 | tf_op jit(solution)/shard_map/ppermute | solution.py:30
  19.1 5.1 %collective-permute-start.4 = (bf16[1,64,256]{2,1,0:T(8,128)(2,1)S(1)}, bf16[1,64,256]{2,1,0:T(8,128)(2,1)S(1)}, u32[]{:S(2)}, u32[]{:S(2)}) collective-permute-start(bf16[1,64,256]{2,1,0:T(8,128)(2,1)S(1)} %collective-permute-done.2), channel_id=1, source_target_pairs={{0,4},{4,8},{8,12},{12,16},{16,20},{20,24},{24,28},{28,0},{1,5},{5... | collective-permute-start | bytes 98312 | tf_op jit(solution)/shard_map/ppermute | solution.py:25
  19.1 5.1 %collective-permute-start.5 = (bf16[1,64,256]{2,1,0:T(8,128)(2,1)S(1)}, bf16[1,64,256]{2,1,0:T(8,128)(2,1)S(1)}, u32[]{:S(2)}, u32[]{:S(2)}) collective-permute-start(bf16[1,64,256]{2,1,0:T(8,128)(2,1)S(1)} %collective-permute-done.3), channel_id=1, source_target_pairs={{0,28},{4,0},{8,4},{12,8},{16,12},{20,16},{24,20},{28,24},{1,29},{... | collective-permute-start | bytes 98312 | tf_op jit(solution)/shard_map/ppermute | solution.py:30
  24.3 5.1 %collective-permute-start.6 = (bf16[1,64,256]{2,1,0:T(8,128)(2,1)S(1)}, bf16[1,64,256]{2,1,0:T(8,128)(2,1)S(1)}, u32[]{:S(2)}, u32[]{:S(2)}) collective-permute-start(bf16[1,64,256]{2,1,0:T(8,128)(2,1)S(1)} %collective-permute-done.4), channel_id=1, source_target_pairs={{0,4},{4,8},{8,12},{12,16},{16,20},{20,24},{24,28},{28,0},{1,5},{5... | collective-permute-start | bytes 98312 | tf_op jit(solution)/shard_map/ppermute | solution.py:25
  24.3 47.2 %copy-start = (bf16[3,1,256,256]{3,2,1,0:T(8,128)(2,1)S(1)}, bf16[3,1,256,256]{3,2,1,0:T(8,128)(2,1)}, u32[]{:S(2)}) copy-start(bf16[3,1,256,256]{3,2,1,0:T(8,128)(2,1)} %param.9) | copy-start | bytes 1179652
  30.0 41.6 %copy-start.2 = (bf16[3,1,64,256]{3,2,1,0:T(8,128)(2,1)S(1)}, bf16[3,1,64,256]{3,2,1,0:T(8,128)(2,1)}, u32[]{:S(2)}) copy-start(bf16[3,1,64,256]{3,2,1,0:T(8,128)(2,1)} %param.8) | copy-start | bytes 294916
  30.8 103.5 %all-reduce.9.cloned.1.call-start = ((), (), s32[]{:S(2)}) async-start(), calls=%async_computation.1 | async-start | bytes 131072 | tf_op jit(solution)/shard_map/psum | solution.py:72
  72.6 5.3 %collective-permute-start.7 = (bf16[1,64,256]{2,1,0:T(8,128)(2,1)S(1)}, bf16[1,64,256]{2,1,0:T(8,128)(2,1)S(1)}, u32[]{:S(2)}, u32[]{:S(2)}) collective-permute-start(bf16[1,64,256]{2,1,0:T(8,128)(2,1)S(1)} %get-tuple-element.10), channel_id=1, source_target_pairs={{0,4},{4,8},{8,12},{12,16},{16,20},{20,24},{24,28},{28,0},{1,5},{5... | collective-permute-start | bytes 98312 | tf_op jit(solution)/shard_map/ppermute | solution.py:25
  72.7 5.2 %collective-permute-start.8 = (bf16[1,64,256]{2,1,0:T(8,128)(2,1)S(1)}, bf16[1,64,256]{2,1,0:T(8,128)(2,1)S(1)}, u32[]{:S(2)}, u32[]{:S(2)}) collective-permute-start(bf16[1,64,256]{2,1,0:T(8,128)(2,1)S(1)} %get-tuple-element.10), channel_id=1, source_target_pairs={{0,28},{4,0},{8,4},{12,8},{16,12},{20,16},{24,20},{28,24},{1,29},{... | collective-permute-start | bytes 98312 | tf_op jit(solution)/shard_map/ppermute | solution.py:30
  77.9 5.5 %collective-permute-start.9 = (bf16[1,64,256]{2,1,0:T(8,128)(2,1)S(1)}, bf16[1,64,256]{2,1,0:T(8,128)(2,1)S(1)}, u32[]{:S(2)}, u32[]{:S(2)}) collective-permute-start(bf16[1,64,256]{2,1,0:T(8,128)(2,1)S(1)} %collective-permute-done.7), channel_id=1, source_target_pairs={{0,4},{4,8},{8,12},{12,16},{16,20},{20,24},{24,28},{28,0},{1,5},{5... | collective-permute-start | bytes 98312 | tf_op jit(solution)/shard_map/ppermute | solution.py:25
  77.9 5.5 %collective-permute-start.10 = (bf16[1,64,256]{2,1,0:T(8,128)(2,1)S(1)}, bf16[1,64,256]{2,1,0:T(8,128)(2,1)S(1)}, u32[]{:S(2)}, u32[]{:S(2)}) collective-permute-start(bf16[1,64,256]{2,1,0:T(8,128)(2,1)S(1)} %collective-permute-done.8), channel_id=1, source_target_pairs={{0,28},{4,0},{8,4},{12,8},{16,12},{20,16},{24,20},{28,24},{1,29},{... | collective-permute-start | bytes 98312 | tf_op jit(solution)/shard_map/ppermute | solution.py:30
  83.4 5.1 %collective-permute-start.11 = (bf16[1,64,256]{2,1,0:T(8,128)(2,1)S(1)}, bf16[1,64,256]{2,1,0:T(8,128)(2,1)S(1)}, u32[]{:S(2)}, u32[]{:S(2)}) collective-permute-start(bf16[1,64,256]{2,1,0:T(8,128)(2,1)S(1)} %collective-permute-done.9), channel_id=1, source_target_pairs={{0,4},{4,8},{8,12},{12,16},{16,20},{20,24},{24,28},{28,0},{1,5},{5... | collective-permute-start | bytes 98312 | tf_op jit(solution)/shard_map/ppermute | solution.py:25
  83.4 5.2 %collective-permute-start.12 = (bf16[1,64,256]{2,1,0:T(8,128)(2,1)S(1)}, bf16[1,64,256]{2,1,0:T(8,128)(2,1)S(1)}, u32[]{:S(2)}, u32[]{:S(2)}) collective-permute-start(bf16[1,64,256]{2,1,0:T(8,128)(2,1)S(1)} %collective-permute-done.10), channel_id=1, source_target_pairs={{0,28},{4,0},{8,4},{12,8},{16,12},{20,16},{24,20},{28,24},{1,29},{... | collective-permute-start | bytes 98312 | tf_op jit(solution)/shard_map/ppermute | solution.py:30
  88.5 5.1 %collective-permute-start.13 = (bf16[1,64,256]{2,1,0:T(8,128)(2,1)S(1)}, bf16[1,64,256]{2,1,0:T(8,128)(2,1)S(1)}, u32[]{:S(2)}, u32[]{:S(2)}) collective-permute-start(bf16[1,64,256]{2,1,0:T(8,128)(2,1)S(1)} %collective-permute-done.11), channel_id=1, source_target_pairs={{0,4},{4,8},{8,12},{12,16},{16,20},{20,24},{24,28},{28,0},{1,5},{5... | collective-permute-start | bytes 98312 | tf_op jit(solution)/shard_map/ppermute | solution.py:25
  95.1 96.5 %all-reduce.11.cloned.1.call-start = ((), (), s32[]{:S(2)}) async-start(), calls=%async_computation.2 | async-start | bytes 262144 | tf_op jit(solution)/shard_map/psum | solution.py:93
  136.4 98.8 %all-reduce.13.cloned.1.call-start = ((), (), s32[]{:S(2)}) async-start(), calls=%async_computation.3 | async-start | bytes 131072 | tf_op jit(solution)/shard_map/psum | solution.py:9
  193.1 99.3 %all-reduce.15.cloned.1.call-start = ((), (), s32[]{:S(2)}) async-start(), calls=%async_computation.4 | async-start | bytes 262144 | tf_op jit(solution)/shard_map/psum | solution.py:93
  237.2 98.8 %all-reduce.17.cloned.1.call-start = ((), (), s32[]{:S(2)}) async-start(), calls=%async_computation.5 | async-start | bytes 131072 | tf_op jit(solution)/shard_map/psum | solution.py:9
Sparse Core Ops, SparseCore 0:
  31.0 40.5 all-reduce.6
  95.2 39.0 all-reduce.8
  136.6 54.9 all-reduce.10
  194.3 40.8 all-reduce.12
  237.4 54.9 all-reduce.14
  295.1 40.8 all-reduce.16
